TPU v7x, 256 devices: a whole 4x4x8 slice. The times are simulated.
256 devices in a mesh: group: 8 (over x, core), expert: 32 (over z, y).
Axes of the slice: x: 4, y: 4, z: 8, core: 2. Of those that a mesh axis runs over, the one named last changes fastest.
Arguments:
- out_grad: bfloat16 [65536, 3584], P(('group', 'expert')), may hold values from -6 to 6
- gates: float32 [65536, 8], P(('group', 'expert')), may hold values from 0.05 to 0.6
- routes: int32 [65536, 8], P(('group', 'expert')), may hold values from 0 to 95, all different within a row
- copy_pick: int32 [65536, 8], P(('group', 'expert')), may hold values from 0 to 839
- replica_plan: int32 [32], replicated, may hold values from 0 to 23, as said below
- down_weight: bfloat16 [32, 1024, 3584], P('expert'), as said below
- saved_hidden: bfloat16 [8, 32, 32, 20, 1024], P('group', 'expert'), may hold values from -0.75 to 0.75
Outputs:
- route_grad: float32 [65536, 8], P(('group', 'expert'))
- hidden_grad: bfloat16 [8, 32, 32, 20, 1024], P('group', 'expert')
- copy_grad: bfloat16 [32, 1024, 3584], P('expert', 'group')
Inputs may be any that keep to these rules, and one draw needn't show every extreme that they name: `replica_plan`: every expert 0 to 23 is served by at least one slot; exactly 2 experts are served by more than one slot. `down_weight`: slots that serve the same expert hold equal weights.
All inputs are finite; a program needn't handle non-finite values.
Results may differ from a plain program's by a relative error of at most 0.019.
Values may be sent and summed in bfloat16 or wider, within the bound.
A program may use at most 128 MiB of HBM per device.

v0:
```python
import jax
import jax.numpy as jnp
from jax import lax
from jax.sharding import PartitionSpec as P

HOT = 2


def slot_layout(replica_plan):
    slot_count = replica_plan.shape[0]
    slot_ids = jnp.arange(slot_count, dtype=jnp.int32)
    same_expert = replica_plan[:, None] == replica_plan[None, :]
    earlier_slot = slot_ids[None, :] < slot_ids[:, None]
    ordinal = jnp.sum(same_expert & earlier_slot, axis=1)
    return (slot_ids, same_expert, ordinal)


def route_slots(routes, copy_pick, replica_plan, expert_count):
    slot_ids, same_expert, ordinal = slot_layout(replica_plan)
    serves = replica_plan == routes[..., None]
    copies = jnp.sum(serves, axis=-1)
    inside = routes < expert_count
    chosen = copy_pick % jnp.maximum(copies, 1)
    slot_match = serves & (ordinal == chosen[..., None]) & inside[..., None]
    slot_of = jnp.sum(jnp.where(slot_match, slot_ids, 0), axis=-1)
    return (slot_match, slot_of, inside)


def route_ranks(slot_match):
    onehot = slot_match.astype(jnp.int32)
    earlier = jnp.cumsum(onehot, axis=-2) - onehot
    return jnp.sum(earlier * onehot, axis=-1)


def local(out_grad, gates, routes, copy_pick, replica_plan, down_weight, saved_hidden):
    slot_count = replica_plan.shape[0]
    cap_rows = saved_hidden.shape[3]
    expert_count = slot_count - slot_count // 4
    tok_dev, top_count = routes.shape
    model_width = out_grad.shape[1]
    hidden_units = down_weight.shape[1]
    route_count = tok_dev * top_count
    held_count = slot_count * cap_rows
    slot_match, slot_of, inside = route_slots(routes, copy_pick, replica_plan, expert_count)
    route_rank = route_ranks(slot_match.reshape(route_count, slot_count))
    kept_route = inside.reshape(-1) & (route_rank < cap_rows)
    position = jnp.where(kept_route, slot_of.reshape(-1) * cap_rows + route_rank, held_count)
    source_route = (
        jnp.full((held_count,), route_count, jnp.int32)
        .at[position]
        .set(jnp.arange(route_count, dtype=jnp.int32), mode="drop")
    )
    occupied = source_route < route_count
    safe_route = jnp.where(occupied, source_route, 0)
    grad_held = jnp.where(occupied[:, None], out_grad[safe_route // top_count], 0)
    gate_held = jnp.where(occupied, gates.reshape(-1)[safe_route], 0.0).astype(jnp.bfloat16)
    grad_held = grad_held.reshape(slot_count, cap_rows, model_width)
    gate_held = gate_held.reshape(slot_count, cap_rows)
    got_rows, got_gate = (
        lax.all_to_all(grad_held, "expert", split_axis=0, concat_axis=0, tiled=True),
        lax.all_to_all(gate_held, "expert", split_axis=0, concat_axis=0, tiled=True),
    )
    flat_rows = got_rows.reshape(held_count, model_width)
    gate_f = got_gate.reshape(held_count, 1).astype(jnp.float32)
    held_hidden = saved_hidden.reshape(held_count, hidden_units)
    projected = lax.dot_general(
        flat_rows, down_weight[0], (((1,), (1,)), ((), ())), preferred_element_type=jnp.float32
    )
    hidden_grad = (gate_f * projected).astype(jnp.bfloat16)
    route_score = jnp.sum(projected * held_hidden.astype(jnp.float32), axis=1)
    returned = lax.all_to_all(
        route_score.reshape(slot_count, cap_rows), "expert", split_axis=0, concat_axis=0, tiled=True
    )
    score_flat = jnp.concatenate([returned.reshape(-1), jnp.zeros((1,), jnp.float32)])
    route_grad = jnp.where(kept_route, score_flat[position], 0.0).reshape(tok_dev, top_count)
    scaled = (gate_f * flat_rows.astype(jnp.float32)).astype(jnp.bfloat16)
    shard_rows = hidden_units // lax.axis_size("group")
    group_sum = lax.psum_scatter(
        lax.dot_general(
            held_hidden, scaled, (((0,), (0,)), ((), ())), preferred_element_type=jnp.float32
        ).astype(jnp.bfloat16),
        "group",
        scatter_dimension=0,
        tiled=True,
    )
    slot_ids, same_expert, ordinal = slot_layout(replica_plan)
    copies = jnp.sum(same_expert, axis=1)
    hot_first = (copies > 1) & (ordinal == 0)
    hot_rank = jnp.sum(hot_first[None, :] & (replica_plan[None, :] < replica_plan[:, None]), axis=1)
    my_slot = slot_ids == lax.axis_index("expert")
    my_rank = jnp.sum(jnp.where(my_slot, hot_rank, 0))
    my_hot = jnp.any(my_slot & (copies > 1))
    hot_ids = jnp.arange(HOT, dtype=jnp.int32)
    place_hot = (hot_ids == my_rank) & my_hot
    group_f = group_sum.astype(jnp.float32)
    table = jnp.where(place_hot[:, None, None], group_f[None], 0.0)
    summed = lax.psum(table.astype(jnp.bfloat16), "expert").astype(jnp.float32)
    picked = jnp.sum(jnp.where(place_hot[:, None, None], summed, 0.0), axis=0)
    copy_grad = jnp.where(my_hot, picked, group_f).astype(jnp.bfloat16)
    hidden_out = hidden_grad.reshape(1, 1, slot_count, cap_rows, hidden_units)
    return (route_grad, hidden_out, copy_grad.reshape(1, shard_rows, model_width))


def solution(mesh):
    placed = (
        P(("group", "expert"), None),
        P(("group", "expert"), None),
        P(("group", "expert"), None),
        P(("group", "expert"), None),
        P(),
        P("expert", None, None),
        P("group", "expert", None, None, None),
    )
    return jax.shard_map(
        local,
        mesh=mesh,
        in_specs=placed,
        out_specs=(
            P(("group", "expert"), None),
            P("group", "expert", None, None, None),
            P("expert", "group", None),
        ),
        check_vma=False,
    )
```

profile of v0, /device:TPU:2, one launch (start us, length us, event | category | flops | bytes accessed | tf_op | source)
XLA Modules:
  0.0 451.8 jit_solution(13898555410454085809)
XLA Ops:
  14.6 9.1 %reduce-window.6 = s32[32,16,128]{2,1,0:T(8,128)S(1)} reduce-window(s32[32,16,128]{2,1,0:T(8,128)S(1)} %and_convert_fusion, s32[]{:T(128)} %constant.17.clone.1), window={size=1x1x128 pad=0_0x0_0x127_0}, to_apply=%region_2.3 | reduce-window | flops 8323072 | bytes 524292 | tf_op jit(solution)/shard_map/reduce-window
  25.3 8.0 %scatter_custom_fusion = s32[640]{0:T(1024)S(1)} fusion(s32[2048]{0:T(1024)S(1)} %bitcast.45, s32[2048]{0:T(1024)S(1)} %iota.19, s32[]{:T(128)} %constant.20.clone.1), kind=kCustom, calls=%fused_computation.57 | custom fusion | bytes 2564 | tf_op jit(solution)/shard_map/scatter | solution.py:51
  33.3 4.3 gather_fusion.2
  38.4 11.5 %all-to-all-start.2 = ((bf16[32,1,20]{2,1,0:T(2,128)(2,1)}), bf16[32,1,20]{2,1,0:T(2,128)(2,1)S(1)}, u32[]{:S(2)}, u32[]{:S(2)}) async-start(bf16[32,1,20]{2,1,0:T(2,128)(2,1)} %all_to_all.20), calls=%async_computation.2 | async-start | bytes 32768 | tf_op jit(solution)/shard_map/all_to_all | solution.py:61
  50.0 5.1 %gather_fusion = bf16[640,3584]{1,0:T(8,128)(2,1)} fusion(bf16[256,3584]{1,0:T(8,128)(2,1)S(1)} %copy-done, s32[1024]{0:T(1024)S(1)} %pad_clamp_fusion.1), kind=kCustom, calls=%fused_computation | custom fusion | bytes 9177600 | tf_op jit(solution)/shard_map/gather | solution.py:55
  55.1 7.3 %gather.14 = bf16[32,20,3584]{2,1,0:T(8,128)(2,1)} reshape(bf16[640,3584]{1,0:T(8,128)(2,1)} %gather_fusion) | data formatting | bytes 9175040 | tf_op jit(solution)/shard_map/gather | solution.py:55
  62.4 5.4 %broadcast_select_fusion = bf16[32,20,3584]{2,1,0:T(8,128)(2,1)} fusion(bf16[32,20,3584]{2,1,0:T(8,128)(2,1)} %gather.14, pred[32,20]{1,0:T(8,128)(4,1)S(1)} %broadcast_in_dim.101), kind=kLoop, calls=%fused_computation.9 | loop fusion | flops 2293760 | bytes 9175680 | tf_op jit(solution)/shard_map/jit(_where)/select_n | solution.py:55
  67.9 9.9 %all-to-all-start = ((bf16[32,20,3584]{2,1,0:T(8,128)(2,1)}), bf16[32,20,3584]{2,1,0:T(8,128)(2,1)}, u32[]{:S(2)}, u32[]{:S(2)}) async-start(bf16[32,20,3584]{2,1,0:T(8,128)(2,1)} %broadcast_select_fusion), calls=%async_computation | async-start | bytes 11010048 | tf_op jit(solution)/shard_map/all_to_all | solution.py:60
  78.0 2.1 copy.58
  81.3 118.0 %all-to-all-done = bf16[32,20,3584]{2,1,0:T(8,128)(2,1)} async-done(((bf16[32,20,3584]{2,1,0:T(8,128)(2,1)}), bf16[32,20,3584]{2,1,0:T(8,128)(2,1)}, u32[]{:S(2)}, u32[]{:S(2)}) %all-to-all-start) | async-done | bytes 4587552 | tf_op jit(solution)/shard_map/all_to_all | solution.py:60
  199.3 6.8 %multiply_convert_fusion = bf16[32,20,3584]{2,1,0:T(8,128)(2,1)} fusion(bf16[32,20,3584]{2,1,0:T(8,128)(2,1)} %all-to-all-done, f32[32,20]{1,0:T(8,128)S(1)} %bitcast.41), kind=kLoop, calls=%fused_computation.4 | loop fusion | flops 6881280 | bytes 9177600 | tf_op jit(solution)/shard_map/convert_element_type | solution.py:76
  206.0 7.4 %convert_element_type.91 = bf16[640,3584]{1,0:T(8,128)(2,1)} reshape(bf16[32,20,3584]{2,1,0:T(8,128)(2,1)} %multiply_convert_fusion) | data formatting | bytes 9175040 | tf_op jit(solution)/shard_map/convert_element_type | solution.py:76
  213.4 10.3 %fusion.2 = bf16[1024,3584]{0,1:T(8,128)(2,1)} fusion(bf16[640,3584]{1,0:T(8,128)(2,1)} %convert_element_type.91, bf16[640,1024]{1,0:T(8,128)(2,1)S(1)} %copy-done.3), kind=kOutput, calls=%fused_computation.8 | convolution fusion | flops 4701290496 | bytes 13238272 | tf_op jit(solution)/shard_map/dot_general | solution.py:79
  223.7 10.1 %copy.66 = bf16[1024,3584]{1,0:T(8,128)(2,1)} copy(bf16[1024,3584]{0,1:T(8,128)(2,1)} %fusion.2) | data formatting | bytes 14680064
  236.7 7.3 %reshape.192 = bf16[640,3584]{1,0:T(8,128)(2,1)} reshape(bf16[32,20,3584]{2,1,0:T(8,128)(2,1)} %all-to-all-done) | data formatting | bytes 9175040 | tf_op jit(solution)/shard_map/reshape | solution.py:63
  244.0 38.6 %reduce-scatter.4.cloned.1.call-done = bf16[128,3584]{1,0:T(8,128)(2,1)} async-done(((bf16[1024,3584]{1,0:T(8,128)(2,1)}), bf16[128,3584]{1,0:T(8,128)(2,1)}) %reduce-scatter.4.cloned.1.call-update) | async-done | bytes 917520 | tf_op jit(solution)/shard_map/reduce_scatter | solution.py:78
  282.6 2.7 select_convert_fusion
  285.4 10.5 %multiply_convert_fusion.1 = (bf16[640,1024]{1,0:T(8,128)(2,1)}, f32[640]{0:T(1024)S(1)}) fusion(f32[640]{0:T(1024)S(1)} %reshape.198, bf16[640,1024]{1,0:T(8,128)(2,1)S(1)} %copy-done.3, bf16[640,3584]{1,0:T(8,128)(2,1)} %reshape.192, bf16[1,1024,3584]{2,1,0:T(8,128)(2,1)} %param.12), kind=kOutput, calls=%fused_computation.12 | convolution fusion | flops 4700896768 | bytes 14554112 | tf_op jit(solution)/shard_map/dot_general | solution.py:66
  296.6 10.1 %all-to-all-start.1 = ((f32[32,1,20]{2,1,0:T(1,128)}), f32[32,1,20]{2,1,0:T(1,128)S(1)}, u32[]{:S(2)}, u32[]{:S(2)}) async-start(f32[32,1,20]{2,1,0:T(1,128)} %bitcast.6), calls=%async_computation.1 | async-start | bytes 32768 | tf_op jit(solution)/shard_map/all_to_all | solution.py:71
  306.8 2.2 reshape.196
  310.8 5.6 %all-to-all-done.1 = f32[32,1,20]{2,1,0:T(1,128)S(1)} async-done(((f32[32,1,20]{2,1,0:T(1,128)}), f32[32,1,20]{2,1,0:T(1,128)S(1)}, u32[]{:S(2)}, u32[]{:S(2)}) %all-to-all-start.1) | async-done | bytes 2592 | tf_op jit(solution)/shard_map/all_to_all | solution.py:71
  317.8 8.6 %gather_fusion.1 = f32[2048]{0:T(1024)S(1)} fusion(f32[641]{0:T(1024)S(1)} %pad_maximum_fusion, s32[2048]{0:T(1024)S(1)} %broadcast_clamp_fusion), kind=kCustom, calls=%fused_computation.1 | custom fusion | bytes 24576 | tf_op jit(solution)/shard_map/gather | solution.py:75
  327.2 114.1 %all-reduce.2.cloned.1.call-done = bf16[2,128,3584]{2,1,0:T(8,128)(2,1)} async-done(((bf16[2,128,3584]{2,1,0:T(8,128)(2,1)}), bf16[2,128,3584]{2,1,0:T(8,128)(2,1)}) %all-reduce.2.cloned.1.call-update) | async-done | bytes 1835024 | tf_op jit(solution)/shard_map/psum | solution.py:97
  441.3 2.0 select_reduce_fusion
  (72 shorter events, 20.5 us)
Async XLA Ops:
  7.2 42.9 %copy-start = (bf16[256,3584]{1,0:T(8,128)(2,1)S(1)}, bf16[256,3584]{1,0:T(8,128)(2,1)}, u32[]{:S(2)}) copy-start(bf16[256,3584]{1,0:T(8,128)(2,1)} %param.7) | copy-start | bytes 5505028
  38.4 29.5 %all-to-all-start.2 = ((bf16[32,1,20]{2,1,0:T(2,128)(2,1)}), bf16[32,1,20]{2,1,0:T(2,128)(2,1)S(1)}, u32[]{:S(2)}, u32[]{:S(2)}) async-start(bf16[32,1,20]{2,1,0:T(2,128)(2,1)} %all_to_all.20), calls=%async_computation.2 | async-start | bytes 32768 | tf_op jit(solution)/shard_map/all_to_all | solution.py:61
  67.9 131.4 %all-to-all-start = ((bf16[32,20,3584]{2,1,0:T(8,128)(2,1)}), bf16[32,20,3584]{2,1,0:T(8,128)(2,1)}, u32[]{:S(2)}, u32[]{:S(2)}) async-start(bf16[32,20,3584]{2,1,0:T(8,128)(2,1)} %broadcast_select_fusion), calls=%async_computation | async-start | bytes 11010048 | tf_op jit(solution)/shard_map/all_to_all | solution.py:60
  77.8 204.9 %reduce-scatter.4.cloned.1.call-start = ((), (), s32[]{:S(2)}) async-start(), calls=%async_computation.5 | async-start | bytes 8257536 | tf_op jit(solution)/shard_map/reduce_scatter | solution.py:78
  206.0 7.4 %copy-start.3 = (bf16[640,1024]{1,0:T(8,128)(2,1)S(1)}, bf16[640,1024]{1,0:T(8,128)(2,1)}, u32[]{:S(2)}) copy-start(bf16[640,1024]{1,0:T(8,128)(2,1)} %reshape.193) | copy-start | bytes 3932164
  233.8 0.7 copy-start.4
  233.9 207.4 %all-reduce.2.cloned.1.call-start = ((), (), s32[]{:S(2)}) async-start(), calls=%async_computation.4 | async-start | bytes 3670016 | tf_op jit(solution)/shard_map/psum | solution.py:97
  296.6 19.8 %all-to-all-start.1 = ((f32[32,1,20]{2,1,0:T(1,128)}), f32[32,1,20]{2,1,0:T(1,128)S(1)}, u32[]{:S(2)}, u32[]{:S(2)}) async-start(f32[32,1,20]{2,1,0:T(1,128)} %bitcast.6), calls=%async_computation.1 | async-start | bytes 32768 | tf_op jit(solution)/shard_map/all_to_all | solution.py:71
  317.7 125.6 %copy-start.2 = (bf16[128,3584]{1,0:T(8,128)(2,1)S(1)}, bf16[128,3584]{1,0:T(8,128)(2,1)}, u32[]{:S(2)}) copy-start(bf16[128,3584]{1,0:T(8,128)(2,1)} %reduce-scatter.4.cloned.1.call-done) | copy-start | bytes 2752516
  317.8 127.3 %copy-start.1 = (bf16[256,3584]{1,0:T(8,128)(2,1)S(1)}, bf16[256,3584]{1,0:T(8,128)(2,1)}, u32[]{:S(2)}) copy-start(bf16[256,3584]{1,0:T(8,128)(2,1)} %param.7) | copy-start | bytes 5505028
Sparse Core Ops, SparseCore 0:
  234.0 48.5 reduce-scatter.3
  286.1 155.1 all-reduce.1
where the time goes:
time: 453 us; the launch traced here: 452 us
  waiting for transfers between devices  276 us (61%)
  local copies, waits for them, and re-layouts  71.8 us (16%)
  other arithmetic  36.7 us (8%)
  starting transfers between devices  31.7 us (7%)
  matrix products  20.8 us (5%)
  between operations  14.4 us (3%)
    all_to_all x1, waiting for transfers between devices, local(): lax.all_to_all(grad_held, 'expert', split_axis=0, concat_axis=0, tiled=True)  118 us
    psum x1, waiting for transfers between devices, local(): summed = lax.psum(table.astype(jnp.bfloat16), 'expert').astype(jnp.float32)  114 us
    reduce_scatter x1, waiting for transfers between devices, local(): lax.psum_scatter(lax.dot_general(held_hidden, scaled, (((0,), (0,)), ((),...  38.6 us
    unnamed x16, local copies, waits for them, and re-layouts  16.3 us
    gather x2, local copies, waits for them, and re-layouts, local(): out_grad[safe_route // top_count]  12.4 us
    all_to_all x1, starting transfers between devices, local(): lax.all_to_all(gate_held, 'expert', split_axis=0, concat_axis=0, tiled=True)  11.5 us
    dot_general x1, matrix products, local(): lax.dot_general(flat_rows, down_weight[0], (((1,), (1,)), ((), ())), pref...  10.5 us
    dot_general x1, matrix products, local(): lax.dot_general(held_hidden, scaled, (((0,), (0,)), ((), ())), preferred_...  10.3 us
  transfers between devices with their start and end apart: 5, of which 4 were waited for; matrix products, arithmetic and copies ran while one was open for 13% of the time, Pallas kernels for 0%

commit v1 on v0

--- a/solution.py
+++ b/solution.py
@@ -94,7 +94,8 @@
     place_hot = (hot_ids == my_rank) & my_hot
     group_f = group_sum.astype(jnp.float32)
     table = jnp.where(place_hot[:, None, None], group_f[None], 0.0)
-    summed = lax.psum(table.astype(jnp.bfloat16), "expert").astype(jnp.float32)
+    test_circles = lambda field_in, mesh_dim: jnp.sum(lax.all_gather(field_in, mesh_dim), axis=0)
+    summed = test_circles(table.astype(jnp.bfloat16), mesh_dim="expert").astype(jnp.float32)
     picked = jnp.sum(jnp.where(place_hot[:, None, None], summed, 0.0), axis=0)
     copy_grad = jnp.where(my_hot, picked, group_f).astype(jnp.bfloat16)
     hidden_out = hidden_grad.reshape(1, 1, slot_count, cap_rows, hidden_units)

time: 453 us -> 703 us (1.55)
  waiting for transfers between devices: 276 us -> 507 us
  other arithmetic: 36.7 us -> 57.6 us
    all_gather x0 -> x1, waiting for transfers between devices: none -> 335 us  [local(): lax.all_gather(field_in, mesh_dim)]
    psum x1 -> x0, waiting for transfers between devices: 114 us -> none  [local(): summed = lax.psum(table.astype(jnp.bfloat16), 'expert').astype(jnp.float32)]
    reduce_sum x0 -> x1, other arithmetic: none -> 20.6 us  [local(): jnp.sum(lax.all_gather(field_in, mesh_dim), axis=0)]
    reduce_scatter x1, waiting for transfers between devices: 38.6 us -> 45.9 us  [local(): lax.psum_scatter(lax.dot_general(held_hidden, scaled, (((0,), (0,)), ((),...]
  transfers between devices with their start and end apart: 5 -> 5, of which waited for: 4 -> 4; matrix products, arithmetic and copies ran while one was open for 13% -> 8% of each run, Pallas kernels for 0% -> 0%
where the time goes in v1:
time: 703 us; the launch traced here: 701 us
  waiting for transfers between devices  507 us (72%)
  local copies, waits for them, and re-layouts  69.4 us (10%)
  other arithmetic  57.6 us (8%)
  starting transfers between devices  32.1 us (5%)
  matrix products  20.9 us (3%)
  between operations  14.4 us (2%)
    all_gather x1, waiting for transfers between devices, local(): lax.all_gather(field_in, mesh_dim)  335 us
    all_to_all x1, waiting for transfers between devices, local(): lax.all_to_all(grad_held, 'expert', split_axis=0, concat_axis=0, tiled=True)  120 us
    reduce_scatter x1, waiting for transfers between devices, local(): lax.psum_scatter(lax.dot_general(held_hidden, scaled, (((0,), (0,)), ((),...  45.9 us
    reduce_sum x1, other arithmetic, local(): jnp.sum(lax.all_gather(field_in, mesh_dim), axis=0)  20.6 us
    unnamed x16, local copies, waits for them, and re-layouts  14.9 us
  transfers between devices with their start and end apart: 5, of which 4 were waited for; matrix products, arithmetic and copies ran while one was open for 8% of the time, Pallas kernels for 0%

profile of v1, /device:TPU:2, one launch (start us, length us, event | category | flops | bytes accessed | tf_op | source)
XLA Modules:
  0.0 700.9 jit_solution(4196930401446239520)
XLA Ops:
  14.6 9.1 %reduce-window.6 = s32[32,16,128]{2,1,0:T(8,128)S(1)} reduce-window(s32[32,16,128]{2,1,0:T(8,128)S(1)} %and_convert_fusion, s32[]{:T(128)} %constant.18.clone.1), window={size=1x1x128 pad=0_0x0_0x127_0}, to_apply=%region_2.3 | reduce-window | flops 8323072 | bytes 524292 | tf_op jit(solution)/shard_map/reduce-window
  25.3 8.0 %scatter_custom_fusion = s32[640]{0:T(1024)S(1)} fusion(s32[2048]{0:T(1024)S(1)} %bitcast.45, s32[2048]{0:T(1024)S(1)} %iota.19, s32[]{:T(128)} %constant.23.clone.1), kind=kCustom, calls=%fused_computation.57 | custom fusion | bytes 2564 | tf_op jit(solution)/shard_map/scatter | solution.py:51
  33.3 4.3 gather_fusion.2
  38.4 11.5 %all-to-all-start.2 = ((bf16[32,1,20]{2,1,0:T(2,128)(2,1)}), bf16[32,1,20]{2,1,0:T(2,128)(2,1)S(1)}, u32[]{:S(2)}, u32[]{:S(2)}) async-start(bf16[32,1,20]{2,1,0:T(2,128)(2,1)} %all_to_all.20), calls=%async_computation.2 | async-start | bytes 32768 | tf_op jit(solution)/shard_map/all_to_all | solution.py:61
  50.0 5.1 gather_fusion
  55.2 7.2 %gather.14 = bf16[32,20,3584]{2,1,0:T(8,128)(2,1)} reshape(bf16[640,3584]{1,0:T(8,128)(2,1)} %gather_fusion) | data formatting | bytes 9175040 | tf_op jit(solution)/shard_map/gather | solution.py:55
  62.4 5.4 broadcast_select_fusion
  67.8 10.0 %all-to-all-start = ((bf16[32,20,3584]{2,1,0:T(8,128)(2,1)}), bf16[32,20,3584]{2,1,0:T(8,128)(2,1)}, u32[]{:S(2)}, u32[]{:S(2)}) async-start(bf16[32,20,3584]{2,1,0:T(8,128)(2,1)} %broadcast_select_fusion), calls=%async_computation | async-start | bytes 11010048 | tf_op jit(solution)/shard_map/all_to_all | solution.py:60
  79.1 120.2 %all-to-all-done = bf16[32,20,3584]{2,1,0:T(8,128)(2,1)} async-done(((bf16[32,20,3584]{2,1,0:T(8,128)(2,1)}), bf16[32,20,3584]{2,1,0:T(8,128)(2,1)}, u32[]{:S(2)}, u32[]{:S(2)}) %all-to-all-start) | async-done | bytes 4587552 | tf_op jit(solution)/shard_map/all_to_all | solution.py:60
  199.3 6.7 multiply_convert_fusion
  206.0 7.3 %convert_element_type.100 = bf16[640,3584]{1,0:T(8,128)(2,1)} reshape(bf16[32,20,3584]{2,1,0:T(8,128)(2,1)} %multiply_convert_fusion) | data formatting | bytes 9175040 | tf_op jit(solution)/shard_map/convert_element_type | solution.py:76
  213.3 10.3 %fusion.2 = bf16[1024,3584]{0,1:T(8,128)(2,1)} fusion(bf16[640,3584]{1,0:T(8,128)(2,1)} %convert_element_type.100, bf16[640,1024]{1,0:T(8,128)(2,1)S(1)} %reshape.199), kind=kOutput, calls=%fused_computation.8 | convolution fusion | flops 4701290496 | bytes 13238272 | tf_op jit(solution)/shard_map/dot_general | solution.py:79
  223.6 10.0 %copy.66 = bf16[1024,3584]{1,0:T(8,128)(2,1)} copy(bf16[1024,3584]{0,1:T(8,128)(2,1)} %fusion.2) | data formatting | bytes 14680064
  236.6 45.9 %reduce-scatter.4.cloned.1.call-done = bf16[128,3584]{1,0:T(8,128)(2,1)} async-done(((bf16[1024,3584]{1,0:T(8,128)(2,1)}), bf16[128,3584]{1,0:T(8,128)(2,1)}) %reduce-scatter.4.cloned.1.call-update) | async-done | bytes 917520 | tf_op jit(solution)/shard_map/reduce_scatter | solution.py:78
  282.4 2.8 select_convert_fusion
  285.4 7.3 %reshape.198 = bf16[640,3584]{1,0:T(8,128)(2,1)} reshape(bf16[32,20,3584]{2,1,0:T(8,128)(2,1)} %all-to-all-done) | data formatting | bytes 9175040 | tf_op jit(solution)/shard_map/reshape | solution.py:63
  292.7 10.5 %multiply_convert_fusion.1 = (bf16[640,1024]{1,0:T(8,128)(2,1)}, f32[640]{0:T(1024)S(1)}) fusion(f32[640]{0:T(1024)S(1)} %reshape.204, bf16[640,1024]{1,0:T(8,128)(2,1)S(1)} %reshape.199, bf16[640,3584]{1,0:T(8,128)(2,1)} %reshape.198, bf16[1,1024,3584]{2,1,0:T(8,128)(2,1)} %param.12), kind=kOutput, calls=%fused_computation.12 | convolution fusion | flops 4700896768 | bytes 14554112 | tf_op jit(solution)/shard_map/dot_general | solution.py:66
  303.9 10.3 %all-to-all-start.1 = ((f32[32,1,20]{2,1,0:T(1,128)}), f32[32,1,20]{2,1,0:T(1,128)S(1)}, u32[]{:S(2)}, u32[]{:S(2)}) async-start(f32[32,1,20]{2,1,0:T(1,128)} %bitcast.6), calls=%async_computation.1 | async-start | bytes 32768 | tf_op jit(solution)/shard_map/all_to_all | solution.py:71
  314.4 2.2 reshape.202
  318.4 5.4 all-to-all-done.1
  325.1 8.6 %gather_fusion.1 = f32[2048]{0:T(1024)S(1)} fusion(f32[641]{0:T(1024)S(1)} %pad_maximum_fusion, s32[2048]{0:T(1024)S(1)} %broadcast_clamp_fusion), kind=kCustom, calls=%fused_computation.1 | custom fusion | bytes 24576 | tf_op jit(solution)/shard_map/gather | solution.py:75
  334.5 335.1 %all-gather.2.cloned.1.call-done = bf16[32,2,128,3584]{3,2,1,0:T(8,128)(2,1)} async-done(((bf16[1,2,128,3584]{3,2,1,0:T(8,128)(2,1)}), bf16[32,2,128,3584]{3,2,1,0:T(8,128)(2,1)}) %all-gather.2.cloned.1.call-update) | async-done | bytes 58720272 | tf_op jit(solution)/shard_map/all_gather | solution.py:97
  669.6 20.6 %reduce_sum.108 = bf16[2,128,3584]{2,1,0:T(8,128)(2,1)} reduce(bf16[32,2,128,3584]{3,2,1,0:T(8,128)(2,1)} %all-gather.2.cloned.1.call-done, bf16[]{:T(256)} %constant.51.clone.1), dimensions={0}, to_apply=%region_13.14 | reduce | flops 28442624 | bytes 60555264 | tf_op jit(solution)/shard_map/reduce_sum | solution.py:97
  690.2 2.0 select_reduce_fusion
  (73 shorter events, 20.7 us)
Async XLA Ops:
  7.2 42.9 %copy-start = (bf16[256,3584]{1,0:T(8,128)(2,1)S(1)}, bf16[256,3584]{1,0:T(8,128)(2,1)}, u32[]{:S(2)}) copy-start(bf16[256,3584]{1,0:T(8,128)(2,1)} %param.7) | copy-start | bytes 5505028
  38.4 29.4 %all-to-all-start.2 = ((bf16[32,1,20]{2,1,0:T(2,128)(2,1)}), bf16[32,1,20]{2,1,0:T(2,128)(2,1)S(1)}, u32[]{:S(2)}, u32[]{:S(2)}) async-start(bf16[32,1,20]{2,1,0:T(2,128)(2,1)} %all_to_all.20), calls=%async_computation.2 | async-start | bytes 32768 | tf_op jit(solution)/shard_map/all_to_all | solution.py:61
  67.8 10.3 %copy-start.3 = (bf16[1,1,32,20,1024]{4,2,3,1,0:T(8,128)(2,1)S(1)}, bf16[1,1,32,20,1024]{4,2,3,1,0:T(8,128)(2,1)}, u32[]{:S(2)}) copy-start(bf16[1,1,32,20,1024]{4,2,3,1,0:T(8,128)(2,1)} %param.13) | copy-start | bytes 3932164
  67.8 131.5 %all-to-all-start = ((bf16[32,20,3584]{2,1,0:T(8,128)(2,1)}), bf16[32,20,3584]{2,1,0:T(8,128)(2,1)}, u32[]{:S(2)}, u32[]{:S(2)}) async-start(bf16[32,20,3584]{2,1,0:T(8,128)(2,1)} %broadcast_select_fusion), calls=%async_computation | async-start | bytes 11010048 | tf_op jit(solution)/shard_map/all_to_all | solution.py:60
  77.8 204.6 %reduce-scatter.4.cloned.1.call-start = ((), (), s32[]{:S(2)}) async-start(), calls=%async_computation.5 | async-start | bytes 8257536 | tf_op jit(solution)/shard_map/reduce_scatter | solution.py:78
  233.6 0.8 copy-start.4
  233.7 436.0 %all-gather.2.cloned.1.call-start = ((), (), s32[]{:S(2)}) async-start(), calls=%async_computation.4 | async-start | bytes 60555264 | tf_op jit(solution)/shard_map/all_gather | solution.py:97
  303.9 19.8 %all-to-all-start.1 = ((f32[32,1,20]{2,1,0:T(1,128)}), f32[32,1,20]{2,1,0:T(1,128)S(1)}, u32[]{:S(2)}, u32[]{:S(2)}) async-start(f32[32,1,20]{2,1,0:T(1,128)} %bitcast.6), calls=%async_computation.1 | async-start | bytes 32768 | tf_op jit(solution)/shard_map/all_to_all | solution.py:71
  334.5 357.7 %copy-start.2 = (bf16[128,3584]{1,0:T(8,128)(2,1)S(1)}, bf16[128,3584]{1,0:T(8,128)(2,1)}, u32[]{:S(2)}) copy-start(bf16[128,3584]{1,0:T(8,128)(2,1)} %reduce-scatter.4.cloned.1.call-done) | copy-start | bytes 2752516
  669.6 24.5 %copy-start.1 = (bf16[256,3584]{1,0:T(8,128)(2,1)S(1)}, bf16[256,3584]{1,0:T(8,128)(2,1)}, u32[]{:S(2)}) copy-start(bf16[256,3584]{1,0:T(8,128)(2,1)} %param.7) | copy-start | bytes 5505028
Sparse Core Ops, SparseCore 0:
  233.8 48.6 reduce-scatter.3
  285.4 384.2 all-gather.1
